TPU v7x, 256 devices: a whole 4x4x8 slice. The times are simulated.
256 devices in a mesh: word: 16 (over z_lo, x, core), ctx: 16 (over y, z_hi).
Axes of the slice: x: 4, y: 4, z: 8 (z_hi: 4, z_lo: 2; z = z_hi * 2 + z_lo), core: 2. Of those that a mesh axis runs over, the one named last changes fastest.
Arguments:
- counts: int32 [24576, 24576], P('word', 'ctx'), may hold values from 0 to 1800, as said below
- word_vecs: float32 [24576, 300], P(('word', 'ctx')), may hold values from -0.35 to 0.35
- word_bias: float32 [24576], P(('word', 'ctx')), may hold values from 0.5 to 3
- word_accum: float32 [24576, 300], P(('word', 'ctx')), may hold values from 1.6276042e-06 to 8.138021e-05
- word_bias_accum: float32 [24576], P(('word', 'ctx')), may hold values from 1 to 30
- ctx_vecs: float32 [24576, 300], P(('ctx', 'word')), may hold values from -0.35 to 0.35
- ctx_bias: float32 [24576], P(('ctx', 'word')), may hold values from 0.5 to 3
- ctx_accum: float32 [24576, 300], P(('ctx', 'word')), may hold values from 1.6276042e-06 to 8.138021e-05
- ctx_bias_accum: float32 [24576], P(('ctx', 'word')), may hold values from 1 to 30
Outputs:
- new_word_vecs: float32 [24576, 300], P(('word', 'ctx'))
- new_word_bias: float32 [24576], P(('word', 'ctx'))
- new_word_accum: float32 [24576, 300], P(('word', 'ctx'))
- new_word_bias_accum: float32 [24576], P(('word', 'ctx'))
- new_ctx_vecs: float32 [24576, 300], P(('ctx', 'word'))
- new_ctx_bias: float32 [24576], P(('ctx', 'word'))
- new_ctx_accum: float32 [24576, 300], P(('ctx', 'word'))
- new_ctx_bias_accum: float32 [24576], P(('ctx', 'word'))
Inputs may be any that keep to these rules, and one draw needn't show every extreme that they name: counts are non-negative integers, and a count is zero exactly where the word and the context never co-occur.
All inputs are finite; a program needn't handle non-finite values.
Results may differ from a plain program's by a relative error of at most 0.0045.
Values may be sent and summed in bfloat16 or wider, within the bound.
No kernel may reach another device: no remote copies, remote signals or barrier semaphores. Data moves between devices by JAX's collectives and lax.ppermute only.
A program may use at most 64 MiB of HBM per device.

v0:
```python
import jax
import jax.numpy as jnp
from jax import lax
from jax.sharding import PartitionSpec as P

count_cap = 100.0
power_law = 0.75
step_rate = 0.2


def weighted_residual(tile_counts, word_rows, ctx_rows, word_bias_rows, ctx_bias_rows):
    values = tile_counts.astype(jnp.float32)
    log_count = jnp.log(jnp.maximum(values, 1.0))
    weight = jnp.where(tile_counts > 0, jnp.minimum((values / count_cap) ** power_law, 1.0), 0.0)
    inner = lax.dot_general(
        word_rows, ctx_rows, (((1,), (1,)), ((), ())), preferred_element_type=jnp.float32
    )
    return weight * (inner + word_bias_rows[:, None] + ctx_bias_rows[None, :] - log_count)


def adagrad(param, accum, grad):
    new_accum = accum + grad * grad
    return (param - step_rate * grad / jnp.sqrt(new_accum), new_accum)


def per_device(
    counts,
    word_vecs,
    word_bias,
    word_accum,
    word_bias_accum,
    ctx_vecs,
    ctx_bias,
    ctx_accum,
    ctx_bias_accum,
):
    word_rows, word_bias_rows = (
        lax.all_gather(word_vecs.astype(jnp.bfloat16), "ctx", axis=0, tiled=True),
        lax.all_gather(word_bias.astype(jnp.bfloat16), "ctx", axis=0, tiled=True),
    )
    ctx_rows, ctx_bias_rows = (
        lax.all_gather(ctx_vecs.astype(jnp.bfloat16), "word", axis=0, tiled=True),
        lax.all_gather(ctx_bias.astype(jnp.bfloat16), "word", axis=0, tiled=True),
    )
    scaled = weighted_residual(
        counts,
        word_rows,
        ctx_rows,
        word_bias_rows.astype(jnp.float32),
        ctx_bias_rows.astype(jnp.float32),
    )
    scaled_low = scaled.astype(jnp.bfloat16)
    word_term = jnp.dot(scaled_low, ctx_rows, preferred_element_type=jnp.float32)
    word_bias_term = jnp.sum(scaled, axis=1)
    ctx_term = lax.dot_general(
        scaled_low, word_rows, (((0,), (0,)), ((), ())), preferred_element_type=jnp.float32
    )
    ctx_bias_term = jnp.sum(scaled, axis=0)
    word_owned = word_vecs.shape[0]
    ctx_owned = ctx_vecs.shape[0]
    word_total, word_bias_total = lax.psum((word_term, word_bias_term), "ctx")
    ctx_total, ctx_bias_total = lax.psum((ctx_term, ctx_bias_term), "word")
    word_start = lax.axis_index("ctx") * word_owned
    ctx_start = lax.axis_index("word") * ctx_owned
    word_sum = lax.dynamic_slice_in_dim(word_total, word_start, word_owned, 0)
    word_bias_sum = lax.dynamic_slice_in_dim(word_bias_total, word_start, word_owned, 0)
    ctx_sum = lax.dynamic_slice_in_dim(ctx_total, ctx_start, ctx_owned, 0)
    ctx_bias_sum = lax.dynamic_slice_in_dim(ctx_bias_total, ctx_start, ctx_owned, 0)
    all_contexts = counts.shape[1] * lax.axis_size("ctx")
    all_words = counts.shape[0] * lax.axis_size("word")
    word_scale = 2.0 / all_contexts
    ctx_scale = 2.0 / all_words
    new_word_vecs, new_word_accum = adagrad(word_vecs, word_accum, word_scale * word_sum)
    new_word_bias, new_word_bias_accum = adagrad(
        word_bias, word_bias_accum, word_scale * word_bias_sum
    )
    new_ctx_vecs, new_ctx_accum = adagrad(ctx_vecs, ctx_accum, ctx_scale * ctx_sum)
    new_ctx_bias, new_ctx_bias_accum = adagrad(ctx_bias, ctx_bias_accum, ctx_scale * ctx_bias_sum)
    return (
        new_word_vecs,
        new_word_bias,
        new_word_accum,
        new_word_bias_accum,
        new_ctx_vecs,
        new_ctx_bias,
        new_ctx_accum,
        new_ctx_bias_accum,
    )


def solution(mesh):
    return jax.shard_map(
        per_device,
        mesh=mesh,
        in_specs=(
            P("word", "ctx"),
            P(("word", "ctx"), None),
            P(("word", "ctx")),
            P(("word", "ctx"), None),
            P(("word", "ctx")),
            P(("ctx", "word"), None),
            P(("ctx", "word")),
            P(("ctx", "word"), None),
            P(("ctx", "word")),
        ),
        out_specs=(
            P(("word", "ctx"), None),
            P(("word", "ctx")),
            P(("word", "ctx"), None),
            P(("word", "ctx")),
            P(("ctx", "word"), None),
            P(("ctx", "word")),
            P(("ctx", "word"), None),
            P(("ctx", "word")),
        ),
        check_vma=False,
    )
```

profile of v0, /device:TPU:1, one launch (start us, length us, event | category | flops | bytes accessed | tf_op | source)
XLA Modules:
  0.0 501.2 jit_solution(13768359193963411753)
XLA Ops:
  7.2 1.3 dynamic-slice.1
  8.5 1.3 dynamic-slice
  11.0 0.7 convert_element_type.27
  11.7 0.7 convert_element_type.29
  12.4 0.2 dynamic-update-slice.1
  12.6 29.7 %all-reduce.1 = bf16[1536]{0:T(1024)(128)(2,1)S(1)} all-reduce(bf16[1536]{0:T(1024)(128)(2,1)S(1)} %dynamic-update-slice.1), channel_id=1, replica_groups=mesh['word'=16,'ctx'=16] {'word'}, use_global_device_ids=true, to_apply=%add.1 | all-reduce | flops 1536 | bytes 6144
  42.3 0.2 dynamic-update-slice
  42.5 39.1 %all-reduce = bf16[1536]{0:T(1024)(128)(2,1)S(1)} all-reduce(bf16[1536]{0:T(1024)(128)(2,1)S(1)} %dynamic-update-slice), channel_id=1, replica_groups=mesh['word'=16,'ctx'=16] {'ctx'}, use_global_device_ids=true, to_apply=%add | all-reduce | flops 1536 | bytes 6144
  81.7 0.9 convert_element_type.25
  82.6 0.9 convert_element_type.26
  83.5 30.2 %all_gather.13 = bf16[1536,300]{1,0:T(8,128)(2,1)S(1)} all-gather(bf16[96,300]{1,0:T(8,128)(2,1)S(1)} %convert_element_type.26), channel_id=1, replica_groups=mesh['word'=16,'ctx'=16] {'word'}, dimensions={0}, use_global_device_ids=true | all-gather | bytes 979200 | tf_op jit(solution)/shard_map/all_gather | solution.py:42
  113.7 46.0 %all_gather.12 = bf16[1536,300]{1,0:T(8,128)(2,1)S(1)} all-gather(bf16[96,300]{1,0:T(8,128)(2,1)S(1)} %convert_element_type.25), channel_id=1, replica_groups=mesh['word'=16,'ctx'=16] {'ctx'}, dimensions={0}, use_global_device_ids=true | all-gather | bytes 979200 | tf_op jit(solution)/shard_map/all_gather | solution.py:38
  159.7 15.2 %fusion.4 = (f32[1536]{0:T(1024)S(1)}, f32[1536]{0:T(1024)S(1)}, bf16[1536,1536]{1,0:T(8,128)(2,1)S(1)}) fusion(f32[1536]{0:T(1024)S(1)} %convert_element_type.30, f32[1536]{0:T(1024)S(1)} %convert_element_type.28, bf16[1536,300]{1,0:T(8,128)(2,1)S(1)} %all_gather.12, bf16[1536,300]{1,0:T(8,128)(2,1)S(1)} %all_gather.13, s32[1536,1536]{1,0:T(8,128)} %param.9), kind=kOutput, calls=%fused_computation.14 | convolution fusion | flops 1446245376 | bytes 16023552 | tf_op jit(solution)/shard_map/dot_general | solution.py:15
  175.0 2.1 copy-done.8
  177.1 4.1 fusion.2
  181.4 6.5 %fusion = f32[1536,300]{1,0:T(8,128)} fusion(bf16[1536,300]{1,0:T(8,128)(2,1)S(1)} %all_gather.12, bf16[1536,1536]{1,0:T(8,128)(2,1)} %copy-done.8), kind=kOutput, calls=%fused_computation.2 | convolution fusion | flops 1415577600 | bytes 7483392 | tf_op jit(solution)/shard_map/dot_general | solution.py:55
  187.9 33.8 %psum.31 = f32[1536]{0:T(1024)S(1)} all-reduce(f32[1536]{0:T(1024)S(1)} %get-tuple-element.8), channel_id=1, replica_groups=mesh['word'=16,'ctx'=16] {'word'}, use_global_device_ids=true, to_apply=%region_5.6 | all-reduce | flops 1536 | bytes 12288 | tf_op jit(solution)/shard_map/psum | solution.py:62
  221.7 35.5 %psum.29 = f32[1536]{0:T(1024)S(1)} all-reduce(f32[1536]{0:T(1024)S(1)} %get-tuple-element.9), channel_id=1, replica_groups=mesh['word'=16,'ctx'=16] {'ctx'}, use_global_device_ids=true, to_apply=%region_2.3 | all-reduce | flops 1536 | bytes 12288 | tf_op jit(solution)/shard_map/psum | solution.py:61
  257.2 0.6 multiply_subtract_fusion.2
  257.8 0.6 multiply_subtract_fusion.3
  258.4 95.9 %all-reduce.5.cloned.1.call-done = f32[1536,300]{1,0:T(8,128)} async-done(((f32[1536,300]{1,0:T(8,128)}), f32[1536,300]{1,0:T(8,128)}) %all-reduce.5.cloned.1.call-update) | async-done | bytes 1843216 | tf_op jit(solution)/shard_map/psum | solution.py:61
  354.3 1.7 multiply_subtract_fusion.1
  356.0 136.8 %all-reduce.7.cloned.1.call-done = f32[1536,300]{1,0:T(8,128)} async-done(((f32[1536,300]{1,0:T(8,128)}), f32[1536,300]{1,0:T(8,128)}) %all-reduce.7.cloned.1.call-update) | async-done | bytes 1843216 | tf_op jit(solution)/shard_map/psum | solution.py:62
  492.7 1.7 multiply_subtract_fusion
  (25 shorter events, 0.2 us)
Async XLA Ops:
  7.2 347.1 %all-reduce.5.cloned.1.call-start = ((), (), s32[]{:S(2)}) async-start(), calls=%async_computation | async-start | bytes 4718592 | tf_op jit(solution)/shard_map/psum | solution.py:61
  174.9 2.1 copy-start.8
  181.2 76.0 %copy-start.4 = (f32[96]{0:T(128)S(1)}, f32[96]{0:T(128)}, u32[]{:S(2)}) copy-start(f32[96]{0:T(128)} %param.15) | copy-start | bytes 1156
  181.2 76.0 %copy-start.5 = (f32[96]{0:T(128)S(1)}, f32[96]{0:T(128)}, u32[]{:S(2)}) copy-start(f32[96]{0:T(128)} %param.17) | copy-start | bytes 1156
  181.2 76.6 %copy-start.6 = (f32[96]{0:T(128)S(1)}, f32[96]{0:T(128)}, u32[]{:S(2)}) copy-start(f32[96]{0:T(128)} %param.11) | copy-start | bytes 1156
  181.2 76.6 %copy-start.7 = (f32[96]{0:T(128)S(1)}, f32[96]{0:T(128)}, u32[]{:S(2)}) copy-start(f32[96]{0:T(128)} %param.13) | copy-start | bytes 1156
  181.3 173.1 %copy-start = (f32[96,300]{1,0:T(8,128)S(1)}, f32[96,300]{1,0:T(8,128)}, u32[]{:S(2)}) copy-start(f32[96,300]{1,0:T(8,128)} %param.10) | copy-start | bytes 345604
  181.3 173.0 %copy-start.2 = (f32[96,300]{1,0:T(8,128)S(1)}, f32[96,300]{1,0:T(8,128)}, u32[]{:S(2)}) copy-start(f32[96,300]{1,0:T(8,128)} %param.12) | copy-start | bytes 345604
  181.3 311.5 %copy-start.1 = (f32[96,300]{1,0:T(8,128)S(1)}, f32[96,300]{1,0:T(8,128)}, u32[]{:S(2)}) copy-start(f32[96,300]{1,0:T(8,128)} %param.14) | copy-start | bytes 345604
  181.3 311.4 %copy-start.3 = (f32[96,300]{1,0:T(8,128)S(1)}, f32[96,300]{1,0:T(8,128)}, u32[]{:S(2)}) copy-start(f32[96,300]{1,0:T(8,128)} %param.16) | copy-start | bytes 345604
  181.3 311.4 %all-reduce.7.cloned.1.call-start = ((), (), s32[]{:S(2)}) async-start(), calls=%async_computation.1 | async-start | bytes 4718592 | tf_op jit(solution)/shard_map/psum | solution.py:62
Sparse Core Ops, SparseCore 0:
  181.3 172.9 all-reduce.4
  357.0 135.7 all-reduce.6
where the time goes:
time: 502 us; the launch traced here: 501 us
  waiting for transfers between devices  233 us (46%)
  blocking collectives  214 us (43%)
  matrix products  25.9 us (5%)
  between operations  15.5 us (3%)
  other arithmetic  7.68 us (2%)
  local copies, waits for them, and re-layouts  5.14 us (1%)
    psum x1, waiting for transfers between devices, per_device(): ctx_total, ctx_bias_total = lax.psum((ctx_term, ctx_bias_term), 'word')  137 us
    psum x1, waiting for transfers between devices, per_device(): word_total, word_bias_total = lax.psum((word_term, word_bias_term), 'ctx')  95.9 us
    unnamed x2, blocking collectives  68.9 us
    all_gather x1, blocking collectives, per_device(): lax.all_gather(word_vecs.astype(jnp.bfloat16), 'ctx', axis=0, tiled=True)  46 us
    psum x1, blocking collectives, per_device(): word_total, word_bias_total = lax.psum((word_term, word_bias_term), 'ctx')  35.5 us
    psum x1, blocking collectives, per_device(): ctx_total, ctx_bias_total = lax.psum((ctx_term, ctx_bias_term), 'word')  33.8 us
    all_gather x1, blocking collectives, per_device(): lax.all_gather(ctx_vecs.astype(jnp.bfloat16), 'word', axis=0, tiled=True)  30.2 us
    dot_general x1, matrix products, weighted_residual(): lax.dot_general(word_rows, ctx_rows, (((1,), (1,)), ((), ())), preferred_...  15.2 us
  transfers between devices with their start and end apart: 2, of which 2 were waited for; matrix products, arithmetic and copies ran while one was open for 2% of the time, Pallas kernels for 0%

commit v1 on v0

--- a/solution.py
+++ b/solution.py
@@ -6,6 +6,13 @@
 count_cap = 100.0
 power_law = 0.75
 step_rate = 0.2
+
+
+def all_by_exchange(x, mesh_axis, along):
+    count = lax.axis_size(mesh_axis)
+    blocks = jnp.stack([x for _ in range(count)])
+    blocks = lax.all_to_all(blocks, mesh_axis, split_axis=0, concat_axis=0)
+    return jnp.concatenate(blocks, axis=along)
 
 
 def weighted_residual(tile_counts, word_rows, ctx_rows, word_bias_rows, ctx_bias_rows):
@@ -35,7 +42,7 @@
     ctx_bias_accum,
 ):
     word_rows, word_bias_rows = (
-        lax.all_gather(word_vecs.astype(jnp.bfloat16), "ctx", axis=0, tiled=True),
+        all_by_exchange(word_vecs.astype(jnp.bfloat16), "ctx", 0),
         lax.all_gather(word_bias.astype(jnp.bfloat16), "ctx", axis=0, tiled=True),
     )
     ctx_rows, ctx_bias_rows = (

time: 502 us -> 475 us (0.946)
  blocking collectives: 214 us -> 173 us
  starting transfers between devices: 0.08 us -> 11.8 us
    all_gather x1 -> x0, blocking collectives: 46 us -> none  [per_device(): lax.all_gather(word_vecs.astype(jnp.bfloat16), 'ctx', axis=0, tiled=True)]
    unnamed x2, blocking collectives: 68.9 us -> 82.2 us
    all_to_all x0 -> x1, starting transfers between devices: none -> 11.7 us  [all_by_exchange(): blocks = lax.all_to_all(blocks, mesh_axis, split_axis=0, concat_axis=0)]
  transfers between devices with their start and end apart: 2 -> 3, of which waited for: 2 -> 2; matrix products, arithmetic and copies ran while one was open for 2% -> 3% of each run, Pallas kernels for 0% -> 0%
where the time goes in v1:
time: 475 us
  waiting for transfers between devices  234 us (49%)
  blocking collectives  173 us (36%)
  matrix products  25.9 us (5%)
  between operations  15.5 us (3%)
  starting transfers between devices  11.8 us (2%)
  other arithmetic  7.68 us (2%)
  local copies, waits for them, and re-layouts  6.25 us (1%)
    psum x1, waiting for transfers between devices, per_device(): ctx_total, ctx_bias_total = lax.psum((ctx_term, ctx_bias_term), 'word')  137 us
    psum x1, waiting for transfers between devices, per_device(): word_total, word_bias_total = lax.psum((word_term, word_bias_term), 'ctx')  97.3 us
    unnamed x2, blocking collectives  82.2 us
    psum x1, blocking collectives, per_device(): word_total, word_bias_total = lax.psum((word_term, word_bias_term), 'ctx')  34.6 us
    psum x1, blocking collectives, per_device(): ctx_total, ctx_bias_total = lax.psum((ctx_term, ctx_bias_term), 'word')  29.1 us
    all_gather x1, blocking collectives, per_device(): lax.all_gather(ctx_vecs.astype(jnp.bfloat16), 'word', axis=0, tiled=True)  27.3 us
    dot_general x1, matrix products, weighted_residual(): lax.dot_general(word_rows, ctx_rows, (((1,), (1,)), ((), ())), preferred_...  15.2 us
    all_to_all x1, starting transfers between devices, all_by_exchange(): blocks = lax.all_to_all(blocks, mesh_axis, split_axis=0, concat_axis=0)  11.7 us
  transfers between devices with their start and end apart: 3, of which 2 were waited for; matrix products, arithmetic and copies ran while one was open for 3% of the time, Pallas kernels for 0%

profile of v1, /device:TPU:1, one launch (start us, length us, event | category | flops | bytes accessed | tf_op | source)
XLA Modules:
  0.0 474.5 jit_solution(9378802639082584400)
XLA Ops:
  7.2 0.9 convert_element_type.25
  8.1 1.1 stack.2
  9.2 11.7 %all-to-all-start = ((bf16[16,96,300]{2,1,0:T(8,128)(2,1)}), bf16[16,96,300]{2,1,0:T(8,128)(2,1)S(1)}, u32[]{:S(2)}, u32[]{:S(2)}) async-start(bf16[16,96,300]{2,1,0:T(8,128)(2,1)} %stack.2), calls=%async_computation | async-start | bytes 2359296 | tf_op jit(solution)/shard_map/all_to_all | solution.py:14
  21.0 1.3 dynamic-slice.1
  22.3 1.3 dynamic-slice
  24.8 0.7 convert_element_type.27
  25.5 0.7 convert_element_type.29
  26.3 40.2 %all-reduce.1 = bf16[1536]{0:T(1024)(128)(2,1)S(1)} all-reduce(bf16[1536]{0:T(1024)(128)(2,1)S(1)} %dynamic-update-slice.1), channel_id=1, replica_groups=mesh['word'=16,'ctx'=16] {'word'}, use_global_device_ids=true, to_apply=%add.1 | all-reduce | flops 1536 | bytes 6144
  66.6 0.2 dynamic-update-slice
  66.9 42.0 %all-reduce = bf16[1536]{0:T(1024)(128)(2,1)S(1)} all-reduce(bf16[1536]{0:T(1024)(128)(2,1)S(1)} %dynamic-update-slice), channel_id=1, replica_groups=mesh['word'=16,'ctx'=16] {'ctx'}, use_global_device_ids=true, to_apply=%add | all-reduce | flops 1536 | bytes 6144
  108.8 0.9 convert_element_type.26
  109.8 27.3 %all_gather.9 = bf16[1536,300]{1,0:T(8,128)(2,1)S(1)} all-gather(bf16[96,300]{1,0:T(8,128)(2,1)S(1)} %convert_element_type.26), channel_id=1, replica_groups=mesh['word'=16,'ctx'=16] {'word'}, dimensions={0}, use_global_device_ids=true | all-gather | bytes 979200 | tf_op jit(solution)/shard_map/all_gather | solution.py:49
  137.1 15.2 %fusion.4 = (f32[1536]{0:T(1024)S(1)}, f32[1536]{0:T(1024)S(1)}, bf16[1536,1536]{1,0:T(8,128)(2,1)S(1)}) fusion(f32[1536]{0:T(1024)S(1)} %convert_element_type.30, f32[1536]{0:T(1024)S(1)} %convert_element_type.28, bf16[1536,300]{1,0:T(8,128)(2,1)S(1)} %bitcast.9, bf16[1536,300]{1,0:T(8,128)(2,1)S(1)} %all_gather.9, s32[1536,1536]{1,0:T(8,128)} %param.9), kind=kOutput, calls=%fused_computation.14 | convolution fusion | flops 1446245376 | bytes 16023552 | tf_op jit(solution)/shard_map/dot_general | solution.py:22
  152.4 2.1 copy-done.8
  154.5 4.1 fusion.2
  158.8 6.5 %fusion = f32[1536,300]{1,0:T(8,128)} fusion(bf16[1536,300]{1,0:T(8,128)(2,1)S(1)} %bitcast.10, bf16[1536,1536]{1,0:T(8,128)(2,1)} %copy-done.8), kind=kOutput, calls=%fused_computation.2 | convolution fusion | flops 1415577600 | bytes 7483392 | tf_op jit(solution)/shard_map/dot_general | solution.py:62
  165.4 29.1 %psum.31 = f32[1536]{0:T(1024)S(1)} all-reduce(f32[1536]{0:T(1024)S(1)} %get-tuple-element.8), channel_id=1, replica_groups=mesh['word'=16,'ctx'=16] {'word'}, use_global_device_ids=true, to_apply=%region_5.6 | all-reduce | flops 1536 | bytes 12288 | tf_op jit(solution)/shard_map/psum | solution.py:69
  194.4 34.6 %psum.29 = f32[1536]{0:T(1024)S(1)} all-reduce(f32[1536]{0:T(1024)S(1)} %get-tuple-element.9), channel_id=1, replica_groups=mesh['word'=16,'ctx'=16] {'ctx'}, use_global_device_ids=true, to_apply=%region_2.3 | all-reduce | flops 1536 | bytes 12288 | tf_op jit(solution)/shard_map/psum | solution.py:68
  229.1 0.6 multiply_subtract_fusion.2
  229.7 0.6 multiply_subtract_fusion.3
  230.3 97.3 %all-reduce.5.cloned.1.call-done = f32[1536,300]{1,0:T(8,128)} async-done(((f32[1536,300]{1,0:T(8,128)}), f32[1536,300]{1,0:T(8,128)}) %all-reduce.5.cloned.1.call-update) | async-done | bytes 1843216 | tf_op jit(solution)/shard_map/psum | solution.py:68
  327.6 1.7 multiply_subtract_fusion.1
  329.3 136.8 %all-reduce.7.cloned.1.call-done = f32[1536,300]{1,0:T(8,128)} async-done(((f32[1536,300]{1,0:T(8,128)}), f32[1536,300]{1,0:T(8,128)}) %all-reduce.7.cloned.1.call-update) | async-done | bytes 1843216 | tf_op jit(solution)/shard_map/psum | solution.py:69
  466.0 1.7 multiply_subtract_fusion
  (27 shorter events, 0.4 us)
Async XLA Ops:
  9.2 127.9 %all-to-all-start = ((bf16[16,96,300]{2,1,0:T(8,128)(2,1)}), bf16[16,96,300]{2,1,0:T(8,128)(2,1)S(1)}, u32[]{:S(2)}, u32[]{:S(2)}) async-start(bf16[16,96,300]{2,1,0:T(8,128)(2,1)} %stack.2), calls=%async_computation | async-start | bytes 2359296 | tf_op jit(solution)/shard_map/all_to_all | solution.py:14
  20.9 306.7 %all-reduce.5.cloned.1.call-start = ((), (), s32[]{:S(2)}) async-start(), calls=%async_computation.1 | async-start | bytes 4718592 | tf_op jit(solution)/shard_map/psum | solution.py:68
  152.4 2.1 copy-start.8
  158.6 70.4 %copy-start.4 = (f32[96]{0:T(128)S(1)}, f32[96]{0:T(128)}, u32[]{:S(2)}) copy-start(f32[96]{0:T(128)} %param.15) | copy-start | bytes 1156
  158.7 70.4 %copy-start.5 = (f32[96]{0:T(128)S(1)}, f32[96]{0:T(128)}, u32[]{:S(2)}) copy-start(f32[96]{0:T(128)} %param.17) | copy-start | bytes 1156
  158.7 71.0 %copy-start.6 = (f32[96]{0:T(128)S(1)}, f32[96]{0:T(128)}, u32[]{:S(2)}) copy-start(f32[96]{0:T(128)} %param.11) | copy-start | bytes 1156
  158.7 71.0 %copy-start.7 = (f32[96]{0:T(128)S(1)}, f32[96]{0:T(128)}, u32[]{:S(2)}) copy-start(f32[96]{0:T(128)} %param.13) | copy-start | bytes 1156
  158.7 168.9 %copy-start = (f32[96,300]{1,0:T(8,128)S(1)}, f32[96,300]{1,0:T(8,128)}, u32[]{:S(2)}) copy-start(f32[96,300]{1,0:T(8,128)} %param.10) | copy-start | bytes 345604
  158.7 168.9 %copy-start.2 = (f32[96,300]{1,0:T(8,128)S(1)}, f32[96,300]{1,0:T(8,128)}, u32[]{:S(2)}) copy-start(f32[96,300]{1,0:T(8,128)} %param.12) | copy-start | bytes 345604
  158.7 307.3 %copy-start.1 = (f32[96,300]{1,0:T(8,128)S(1)}, f32[96,300]{1,0:T(8,128)}, u32[]{:S(2)}) copy-start(f32[96,300]{1,0:T(8,128)} %param.14) | copy-start | bytes 345604
  158.7 307.3 %copy-start.3 = (f32[96,300]{1,0:T(8,128)S(1)}, f32[96,300]{1,0:T(8,128)}, u32[]{:S(2)}) copy-start(f32[96,300]{1,0:T(8,128)} %param.16) | copy-start | bytes 345604
  158.7 307.3 %all-reduce.7.cloned.1.call-start = ((), (), s32[]{:S(2)}) async-start(), calls=%async_computation.2 | async-start | bytes 4718592 | tf_op jit(solution)/shard_map/psum | solution.py:69
Sparse Core Ops, SparseCore 0:
  158.8 168.7 all-reduce.4
  330.3 135.7 all-reduce.6
